TPU v7x, 32 devices: a whole 2x2x4 slice. The times are simulated.
32 devices in a mesh: pb: 8 (over z, y), ka: 4 (over x, core).
Axes of the slice: x: 2, y: 2, z: 4, core: 2. Of those that a mesh axis runs over, the one named last changes fastest.
Arguments:
- pair_trunk: bfloat16 [384, 384, 128], P('pb', 'ka'), may hold values from -40 to 40
- token_ids: int32 [3, 384], replicated, may hold values from 0 to 422, as said below
- w_rel: bfloat16 [139, 128], replicated, may hold values from -3.5 to 3.5
- cat_gain: float32 [256], replicated, may hold values from 0.1 to 1.9
- w_in: bfloat16 [256, 128], replicated, may hold values from -0.375 to 0.375
- trans_gain: float32 [2, 128], replicated, may hold values from 0.1 to 1.9
- trans_ab: bfloat16 [2, 128, 512], replicated, may hold values from -0.5 to 0.5
- trans_out: bfloat16 [2, 256, 128], replicated, may hold values from -0.375 to 0.375
- bias_gain: float32 [128], replicated, may hold values from 0.1 to 1.9
- w_bias: bfloat16 [128, 16], replicated, may hold values from -1.5 to 1.5
- normed: bfloat16 [8, 384, 768], P(None, 'pb', 'ka'), may hold values from -12 to 12
- w_proj: bfloat16 [4, 768, 768], P(None, None, 'ka'), may hold values from -1 to 1
- output_weight: bfloat16 [768, 768], P('ka'), may hold values from -0.21875 to 0.21875
Outputs:
- pair_cond: bfloat16 [384, 384, 128], P('pb', 'ka')
- update: bfloat16 [8, 384, 768], P(None, 'pb', 'ka')
Inputs may be any that keep to these rules, and one draw needn't show every extreme that they name: `token_ids`: row 0 is a token's residue number, row 1 its chain number, row 2 its entity number. Chain numbers start at 0 and never fall along the tokens; residue numbers never fall within a chain; all tokens of a chain share one entity. The last token's residue number is 422.
All inputs are finite; a program needn't handle non-finite values.
Results may differ from a plain program's by a relative error of at most 0.015.
The roundings to bfloat16 on the way count: a program that leaves them out, or rounds other values in their place, can miss the bound.
Values may be sent and summed in bfloat16 or wider, within the bound.
A program may use at most 64 MiB of HBM per device.

v0:
```python
import math
import jax
import jax.numpy as jnp
from jax import lax
from jax.sharding import PartitionSpec as P

HD = 48
RMAX = 32
SMAX = 2
REL = 139
EPS = 1e-05


def layer_norm(values, scaling):
    average = jnp.mean(values, axis=-1, keepdims=True)
    centered = values - average
    spread = jnp.mean(centered * centered, axis=-1, keepdims=True)
    return centered * lax.rsqrt(spread + EPS) * scaling


def relative_onehot(query_token_ids, key_ids, query_pos, key_pos):
    query_res = query_token_ids[0][:, None]
    key_res = key_ids[0][None, :]
    query_chain = query_token_ids[1][:, None]
    key_chain = key_ids[1][None, :]
    query_entity = query_token_ids[2][:, None]
    key_ent = key_ids[2][None, :]
    same_chain = query_chain == key_chain
    same_res = same_chain & (query_res == key_res)
    same_entity = query_entity == key_ent
    res_bins = 2 * RMAX + 2
    res_bin = jnp.where(same_chain, jnp.clip(query_res - key_res + RMAX, 0, 2 * RMAX), 2 * RMAX + 1)
    token_offset_bin = jnp.where(
        same_res, jnp.clip(query_pos[:, None] - key_pos[None, :] + RMAX, 0, 2 * RMAX), 2 * RMAX + 1
    )
    chain_offset_bin = jnp.where(
        same_entity, jnp.clip(query_chain - key_chain + SMAX, 0, 2 * SMAX), 2 * SMAX + 1
    )
    columns = jnp.arange(REL, dtype=jnp.int32)
    onehot = (columns == res_bin[..., None]) | (columns == (res_bins + token_offset_bin)[..., None])
    onehot = onehot | (columns == (2 * res_bins + chain_offset_bin)[..., None])
    onehot = onehot | (columns == REL - 1) & same_entity[..., None]
    return onehot.astype(jnp.bfloat16)


def condition_block(
    trunk_blk, onehot, w_rel, cat_gain, w_in, trans_gain, trans_ab, trans_out, bias_gain, w_bias
):
    half = trans_out.shape[1]
    relative = jnp.einsum("rkf,fc->rkc", onehot, w_rel, preferred_element_type=jnp.float32)
    joined = jnp.concatenate([trunk_blk.astype(jnp.float32), relative], axis=-1)
    normal_in = layer_norm(joined, cat_gain).astype(jnp.bfloat16)
    pair_state = jnp.einsum("rkf,fc->rkc", normal_in, w_in, preferred_element_type=jnp.float32)
    for layer_idx in range(2):
        normal_tr = layer_norm(pair_state, trans_gain[layer_idx]).astype(jnp.bfloat16)
        gate_up = jnp.einsum(
            "rkc,cf->rkf", normal_tr, trans_ab[layer_idx], preferred_element_type=jnp.float32
        )
        hidden = (jax.nn.silu(gate_up[..., :half]) * gate_up[..., half:]).astype(jnp.bfloat16)
        pair_state = pair_state + jnp.einsum(
            "rkf,fc->rkc", hidden, trans_out[layer_idx], preferred_element_type=jnp.float32
        )
    normal_b = layer_norm(pair_state, bias_gain).astype(jnp.bfloat16)
    bias_blk = jnp.einsum(
        "rkc,ch->hrk", normal_b, w_bias, preferred_element_type=jnp.float32
    ).astype(jnp.bfloat16)
    return (pair_state.astype(jnp.bfloat16), bias_blk)


def soft_weights(logits):
    row_max = jnp.max(logits, axis=-1, keepdims=True)
    expweights = jnp.exp(logits - row_max)
    return (expweights / jnp.sum(expweights, axis=-1, keepdims=True)).astype(jnp.bfloat16)


def shards(
    pair_trunk,
    token_ids,
    w_rel,
    cat_gain,
    w_in,
    trans_gain,
    trans_ab,
    trans_out,
    bias_gain,
    w_bias,
    normed,
    w_proj,
    output_weight,
):
    q_rows = pair_trunk.shape[0]
    k_rows = pair_trunk.shape[1]
    q_start = lax.axis_index("pb") * q_rows
    k_start = lax.axis_index("ka") * k_rows
    key_ids = lax.dynamic_slice_in_dim(token_ids, k_start, k_rows, 1)
    key_pos = k_start + jnp.arange(k_rows, dtype=jnp.int32)
    row_blk = 8

    def one_block(block_idx):
        begin_at = block_idx * row_blk
        trunk_blk = lax.dynamic_slice_in_dim(pair_trunk, begin_at, row_blk, 0)
        query_token_ids = lax.dynamic_slice_in_dim(token_ids, q_start + begin_at, row_blk, 1)
        query_pos = q_start + begin_at + jnp.arange(row_blk, dtype=jnp.int32)
        onehot = relative_onehot(query_token_ids, key_ids, query_pos, key_pos)
        return condition_block(
            trunk_blk,
            onehot,
            w_rel,
            cat_gain,
            w_in,
            trans_gain,
            trans_ab,
            trans_out,
            bias_gain,
            w_bias,
        )

    pair_blocks, bias_blocks = lax.map(one_block, jnp.arange(q_rows // row_blk, dtype=jnp.int32))
    pair_cond = pair_blocks.reshape(q_rows, k_rows, pair_blocks.shape[-1])
    bias_tile = jnp.transpose(bias_blocks, (1, 0, 2, 3)).reshape(
        bias_blocks.shape[1], q_rows, k_rows
    )
    samples = normed.shape[0]
    feat_local = normed.shape[2]
    heads_local = feat_local // HD
    scale_factor = 1.0 / math.sqrt(HD)
    projected = jnp.einsum(
        "sqf,pfe->psqe",
        lax.all_gather(normed, "ka", axis=2, tiled=True),
        w_proj,
        preferred_element_type=jnp.float32,
    )
    queries = projected[0].astype(jnp.bfloat16).reshape(samples, q_rows, heads_local, HD)
    kv_local = jnp.transpose(
        jnp.stack([projected[1], projected[2]], axis=1).astype(jnp.bfloat16), (0, 1, 3, 2)
    )
    bias_rows = lax.all_to_all(bias_tile, "ka", split_axis=0, concat_axis=2, tiled=True)
    kv_all = lax.all_gather(kv_local, "pb", axis=3, tiled=True)
    keys_all = kv_all[:, 0].reshape(samples, heads_local, HD, kv_all.shape[3])
    values_all = kv_all[:, 1].reshape(samples, heads_local, HD, kv_all.shape[3])
    logits = (
        jnp.einsum("sqhd,shdk->shqk", queries, keys_all, preferred_element_type=jnp.float32)
        * scale_factor
    )
    logits = logits + bias_rows[None].astype(jnp.float32)
    weights = soft_weights(logits)
    attended = jnp.einsum(
        "shqk,shdk->sqhd", weights, values_all, preferred_element_type=jnp.float32
    )
    gated_result = (
        attended.reshape(samples, q_rows, feat_local) * jax.nn.sigmoid(projected[3])
    ).astype(jnp.bfloat16)
    flat_gated = gated_result.reshape(samples * q_rows, feat_local)
    summed = lax.psum_scatter(
        jnp.einsum(
            "fe,nf->en", output_weight, flat_gated, preferred_element_type=jnp.float32
        ).astype(jnp.bfloat16),
        "ka",
        scatter_dimension=0,
        tiled=True,
    ).astype(jnp.float32)
    update = jnp.transpose(summed).reshape(samples, q_rows, feat_local).astype(jnp.bfloat16)
    return (pair_cond, update)


def solution(mesh):
    in_specs = (
        P("pb", "ka", None),
        P(),
        P(),
        P(),
        P(),
        P(),
        P(),
        P(),
        P(),
        P(),
        P(None, "pb", "ka"),
        P(None, None, "ka"),
        P("ka", None),
    )
    out_specs = (P("pb", "ka", None), P(None, "pb", "ka"))
    return jax.shard_map(shards, mesh=mesh, in_specs=in_specs, out_specs=out_specs, check_vma=False)
```

profile of v0, /device:TPU:0, one launch (start us, length us, event | category | flops | bytes accessed | tf_op | source)
XLA Modules:
  0.0 148.7 jit_solution(9345763957200801556)
XLA Ops:
  7.2 1.3 copy.25
  8.5 14.3 %all_gather.6 = bf16[8,48,768]{1,0,2:T(8,128)(2,1)S(1)} all-gather(bf16[8,48,192]{1,0,2:T(8,128)(2,1)S(1)} %copy.25), channel_id=1, replica_groups=mesh['pb'=8,'ka'=4] {'ka'}, dimensions={2}, use_global_device_ids=true | all-gather | bytes 737280 | tf_op jit(solution)/shard_map/all_gather | solution.py:129
  22.8 1.6 %copy.26 = bf16[8,48,768]{2,1,0:T(8,128)(2,1)} copy(bf16[8,48,768]{1,0,2:T(8,128)(2,1)S(1)} %all_gather.6) | data formatting | bytes 1179648 | tf_op jit(solution)/shard_map/all_gather | solution.py:129
  24.5 1.8 %fusion.70 = (bf16[4,8,48,192]{3,2,1,0:T(8,128)(2,1)S(1)}, f32[4,8,48,192]{3,2,1,0:T(8,128)S(1)}) fusion(bf16[8,48,768]{2,1,0:T(8,128)(2,1)} %copy.26, bf16[4,768,192]{1,2,0:T(8,128)(2,1)S(1)} %copy-done), kind=kOutput, calls=%fused_computation.118 | convolution fusion | flops 453279744 | bytes 3538944 | tf_op jit(solution)/shard_map/sqf,pfe->psqe/dot_general | solution.py:127
  28.2 60.4 %while.13 = (s32[]{:T(128)}, bf16[6,8,96,128]{3,2,1,0:T(8,128)(2,1)}, bf16[6,16,8,96]{3,1,2,0:T(8,128)(2,1)}, s32[6]{0:T(128)S(1)}, bf16[48,96,128]{2,1,0:T(8,12...) while((s32[]{:T(128)}, ...), condition=%wide.region_10.11_spmd.clone, body=%wide.region_0.10_spmd.clone.sunk | while | flops 390749440 | bytes 15165903 | solution.py:118
  31.4 1.1 fusion.91
  35.6 1.0 bitcast_dynamic-update-slice_fusion.2
  37.2 1.0 fusion.96
  41.5 1.1 fusion.91
  45.7 1.0 bitcast_dynamic-update-slice_fusion.2
  47.3 1.0 fusion.96
  51.6 1.1 fusion.91
  55.7 1.0 bitcast_dynamic-update-slice_fusion.2
  57.4 1.0 fusion.96
  61.6 1.1 fusion.91
  65.8 1.0 bitcast_dynamic-update-slice_fusion.2
  67.4 1.0 fusion.96
  71.7 1.1 fusion.91
  75.9 1.0 bitcast_dynamic-update-slice_fusion.2
  81.8 1.1 fusion.91
  85.9 1.0 bitcast_dynamic-update-slice_fusion.2
  88.6 1.7 %copy.48 = bf16[16,6,8,96]{3,2,1,0:T(8,128)(2,1)} copy(bf16[16,6,8,96]{3,0,2,1:T(8,128)(2,1)} %bitcast.136) | data formatting | bytes 294912 | tf_op jit(solution)/shard_map/transpose | solution.py:120
  90.3 4.0 %all-to-all-start = ((bf16[16,48,96]{2,1,0:T(8,128)(2,1)}), bf16[16,48,96]{2,1,0:T(8,128)(2,1)}, u32[]{:S(2)}, u32[]{:S(2)}) async-start(bf16[16,48,96]{2,1,0:T(8,128)(2,1)} %bitcast.106), calls=%async_computation | async-start | bytes 393216 | tf_op jit(solution)/shard_map/all_to_all | solution.py:137
  96.3 3.3 %all-to-all-done = bf16[16,48,96]{2,1,0:T(8,128)(2,1)} async-done(((bf16[16,48,96]{2,1,0:T(8,128)(2,1)}), bf16[16,48,96]{2,1,0:T(8,128)(2,1)}, u32[]{:S(2)}, u32[]{:S(2)}) %all-to-all-start) | async-done | bytes 147488 | tf_op jit(solution)/shard_map/all_to_all | solution.py:137
  101.8 3.4 %fusion.68 = (bf16[8,1,192,384]{2,3,0,1:T(8,128)(2,1)S(1)}, bf16[8,1,192,384]{2,3,0,1:T(8,128)(2,1)}) fusion(bf16[8,2,192,384]{2,3,0,1:T(8,128)(2,1)} %all-gather.2.cloned.1.call-done), kind=kLoop, calls=%fused_computation.116 | loop fusion | bytes 4718592 | tf_op jit(solution)/shard_map/slice | solution.py:139
  105.1 2.5 %copy.27 = bf16[8,1,192,384]{3,2,0,1:T(8,128)(2,1)} copy(bf16[8,1,192,384]{2,3,0,1:T(8,128)(2,1)} %get-tuple-element.183) | data formatting | bytes 2359296 | tf_op jit(solution)/shard_map/slice | solution.py:140
  107.7 1.5 %copy.28 = bf16[8,1,192,384]{3,2,0,1:T(8,128)(2,1)} copy(bf16[8,1,192,384]{2,3,0,1:T(8,128)(2,1)S(1)} %get-tuple-element.182) | data formatting | bytes 2359296 | tf_op jit(solution)/shard_map/slice | solution.py:139
  109.2 3.6 %fusion.71 = (f32[8,4,48]{2,1,0:T(4,128)S(1)}, f32[8,4,48,384]{3,2,1,0:T(8,128)}) fusion(f32[4,48,384]{2,1,0:T(8,128)} %reshape.365, bf16[8,4,48,384]{3,2,1,0:T(8,128)(2,1)} %bitcast.135, bf16[8,48,4,48]{3,2,1,0:T(4,128)(2,1)S(1)} %copy-done.5), kind=kOutput, calls=%fused_computation.119 | convolution fusion | flops 58982784 | bytes 3987456 | tf_op jit(solution)/shard_map/sub | solution.py:72
  112.8 2.3 %convolution_bitcast_fusion.1 = f32[8,48,4,48]{1,3,2,0:T(8,128)S(1)} fusion(bf16[8,4,48,384]{3,2,1,0:T(8,128)(2,1)S(1)} %bitcast.134, f32[8,4,48,384]{3,2,1,0:T(8,128)} %get-tuple-element.190, f32[8,4,48]{2,1,0:T(4,128)S(1)} %get-tuple-element.189), kind=kOutput, calls=%fused_computation.93 | convolution fusion | flops 57802752 | bytes 3840000 | tf_op jit(solution)/shard_map/shqk,shdk->sqhd/dot_general | solution.py:147
  116.5 1.1 copy.35
  117.6 22.5 %reduce-scatter.4.cloned.1.call-done = bf16[192,384]{1,0:T(8,128)(2,1)} async-done(((bf16[768,384]{1,0:T(8,128)(2,1)}), bf16[192,384]{1,0:T(8,128)(2,1)}) %reduce-scatter.4.cloned.1.call-update) | async-done | bytes 147472
  140.1 1.7 %copy.36 = bf16[192,384]{0,1:T(8,128)(2,1)} copy(bf16[192,384]{1,0:T(8,128)(2,1)} %reduce-scatter.4.cloned.1.call-done) | data formatting | bytes 294912
  (236 shorter events, 46.4 us)
Async XLA Ops:
  7.2 17.3 %copy-start = (bf16[4,768,192]{1,2,0:T(8,128)(2,1)S(1)}, bf16[4,768,192]{1,2,0:T(8,128)(2,1)}, u32[]{:S(2)}) copy-start(bf16[4,768,192]{1,2,0:T(8,128)(2,1)} %param.26) | copy-start | bytes 3538948
  7.2 94.6 %all-gather.2.cloned.1.call-start = ((), (), s32[]{:S(2)}) async-start(), calls=%async_computation.2 | async-start | bytes 3538944 | tf_op jit(solution)/shard_map/all_gather | solution.py:138
  26.3 1.7 %copy-start.9 = (s32[3,384]{1,0:T(4,128)S(1)}, s32[3,384]{1,0:T(4,128)}, u32[]{:S(2)}) copy-start(s32[3,384]{1,0:T(4,128)} %param.16) | copy-start | bytes 13828
  26.3 1.8 %copy-start.1 = (bf16[2,128,512]{2,1,0:T(8,128)(2,1)S(1)}, bf16[2,128,512]{2,1,0:T(8,128)(2,1)}, u32[]{:S(2)}) copy-start(bf16[2,128,512]{2,1,0:T(8,128)(2,1)} %param.21) | copy-start | bytes 786436
  26.4 1.8 %copy-start.7 = (bf16[128,16]{0,1:T(8,128)(2,1)S(1)}, bf16[128,16]{0,1:T(8,128)(2,1)}, u32[]{:S(2)}) copy-start(bf16[128,16]{0,1:T(8,128)(2,1)} %param.24) | copy-start | bytes 12292
  26.4 1.8 %copy-start.8 = (f32[2,128]{1,0:T(2,128)S(1)}, f32[2,128]{1,0:T(2,128)}, u32[]{:S(2)}) copy-start(f32[2,128]{1,0:T(2,128)} %param.20) | copy-start | bytes 3076
  26.4 1.7 %copy-start.10 = (f32[128]{0:T(128)S(1)}, f32[128]{0:T(128)}, u32[]{:S(2)}) copy-start(f32[128]{0:T(128)} %param.23) | copy-start | bytes 1540
  26.4 1.7 %copy-start.12 = (bf16[256,128]{1,0:T(8,128)(2,1)S(1)}, bf16[256,128]{1,0:T(8,128)(2,1)}, u32[]{:S(2)}) copy-start(bf16[256,128]{1,0:T(8,128)(2,1)} %param.19) | copy-start | bytes 196612
  26.4 1.7 %copy-start.13 = (bf16[139,128]{1,0:T(8,128)(2,1)S(1)}, bf16[139,128]{1,0:T(8,128)(2,1)}, u32[]{:S(2)}) copy-start(bf16[139,128]{1,0:T(8,128)(2,1)} %param.17) | copy-start | bytes 106756
  26.4 1.7 %copy-start.14 = (f32[256]{0:T(256)S(1)}, f32[256]{0:T(256)}, u32[]{:S(2)}) copy-start(f32[256]{0:T(256)} %param.18) | copy-start | bytes 3076
  33.5 0.9 copy-start.11
  43.5 0.9 copy-start.11
  53.6 0.9 copy-start.11
  63.7 0.9 copy-start.11
  73.7 0.9 copy-start.11
  83.8 0.9 copy-start.11
  88.6 5.9 %copy-start.4 = (bf16[1,8,48,192]{3,2,1,0:T(8,128)(2,1)S(1)}, bf16[1,8,48,192]{3,2,1,0:T(8,128)(2,1)}, u32[]{:S(2)}) copy-start(bf16[1,8,48,192]{3,2,1,0:T(8,128)(2,1)} %get-tuple-element.184) | copy-start | bytes 442372
  90.3 9.4 %all-to-all-start = ((bf16[16,48,96]{2,1,0:T(8,128)(2,1)}), bf16[16,48,96]{2,1,0:T(8,128)(2,1)}, u32[]{:S(2)}, u32[]{:S(2)}) async-start(bf16[16,48,96]{2,1,0:T(8,128)(2,1)} %bitcast.106), calls=%async_computation | async-start | bytes 393216 | tf_op jit(solution)/shard_map/all_to_all | solution.py:137
  94.3 45.9 %reduce-scatter.4.cloned.1.call-start = ((), (), s32[]{:S(2)}) async-start(), calls=%async_computation.3 | async-start | bytes 737280
  107.7 1.5 %copy-start.5 = (bf16[8,48,4,48]{3,2,1,0:T(4,128)(2,1)S(1)}, bf16[8,48,4,48]{3,2,1,0:T(4,128)(2,1)}, u32[]{:S(2)}) copy-start(bf16[8,48,4,48]{3,2,1,0:T(4,128)(2,1)} %convert_element_type.75) | copy-start | bytes 442372
  109.2 3.7 %copy-start.2 = (bf16[8,1,192,384]{3,2,0,1:T(8,128)(2,1)S(1)}, bf16[8,1,192,384]{3,2,0,1:T(8,128)(2,1)}, u32[]{:S(2)}) copy-start(bf16[8,1,192,384]{3,2,0,1:T(8,128)(2,1)} %copy.27) | copy-start | bytes 3538948
  115.1 1.0 copy-start.3
  115.1 1.1 copy-start.6
Sparse Core Ops, SparseCore 0:
  28.1 60.9 all-gather.1
  117.7 22.3 reduce-scatter.3
where the time goes:
time: 150 us; the launch traced here: 149 us
  matrix products  36 us (24%)
  waiting for transfers between devices  25.9 us (17%)
  other arithmetic  24.9 us (17%)
  local copies, waits for them, and re-layouts  24.6 us (16%)
  blocking collectives  14.3 us (10%)
  between operations  14.3 us (10%)
  loops' own time  4.55 us (3%)
  starting transfers between devices  4.06 us (3%)
    unnamed x3, waiting for transfers between devices  22.6 us
    all_gather x1, blocking collectives, shards(): lax.all_gather(normed, 'ka', axis=2, tiled=True)  14.3 us
    dot_general x12, matrix products, condition_block(): jnp.einsum('rkf,fc->rkc', hidden, trans_out[layer_idx], preferred_element...  8.85 us
    reduce_sum x24, other arithmetic, layer_norm(): spread = jnp.mean(centered * centered, axis=-1, keepdims=True)  8.37 us
    reduce_sum x12, other arithmetic, layer_norm(): average = jnp.mean(values, axis=-1, keepdims=True)  7.67 us
    dot_general x6, matrix products, condition_block(): jnp.einsum('rkc,ch->hrk', normal_b, w_bias, preferred_element_type=jnp.fl...  6.08 us
    convert_element_type x6, other arithmetic, condition_block(): joined = jnp.concatenate([trunk_blk.astype(jnp.float32), relative], axis=-1)  5.75 us
    dot_general x12, matrix products, condition_block(): jnp.einsum('rkc,cf->rkf', normal_tr, trans_ab[layer_idx], preferred_eleme...  5.08 us
  transfers between devices with their start and end apart: 3, of which 2 were waited for; matrix products, arithmetic and copies ran while one was open for 41% of the time, Pallas kernels for 0%

commit v1 on v0

--- a/solution.py
+++ b/solution.py
@@ -9,6 +9,19 @@
 SMAX = 2
 REL = 139
 EPS = 1e-05
+
+
+def end_values(vec, lane_axis):
+    n_all = lax.axis_size(lane_axis)
+    by_place = [vec]
+    for ii in range(1, n_all):
+        u1 = lax.ppermute(
+            by_place[ii - 1], lane_axis, [(idx, (idx - 1) % n_all) for idx in range(n_all)]
+        )
+        by_place.append(u1)
+    value_now = jnp.concatenate(by_place, axis=2)
+    arr_next = lax.axis_index(lane_axis)
+    return jnp.roll(value_now, arr_next * vec.shape[2], axis=2)
 
 
 def layer_norm(values, scaling):
@@ -126,7 +139,7 @@
     scale_factor = 1.0 / math.sqrt(HD)
     projected = jnp.einsum(
         "sqf,pfe->psqe",
-        lax.all_gather(normed, "ka", axis=2, tiled=True),
+        end_values(normed, lane_axis="ka"),
         w_proj,
         preferred_element_type=jnp.float32,
     )

time: 150 us -> 148 us (0.987)
  blocking collectives: 14.3 us -> 8.29 us
  waiting for transfers between devices: 25.9 us -> 31.7 us
  matrix products: 36 us -> 32.6 us
  starting transfers between devices: 4.06 us -> 6.24 us
    all_gather x1 -> x0, blocking collectives: 14.3 us -> none  [shards(): lax.all_gather(normed, 'ka', axis=2, tiled=True)]
    ppermute x0 -> x3, waiting for transfers between devices: none -> 9.12 us  [end_values(): lax.ppermute(by_place[ii - 1], lane_axis, [(idx, (idx - 1) % n_all) for i...]
    all_to_all x0 -> x1, blocking collectives: none -> 8.29 us  [shards(): lax.all_to_all(bias_tile, 'ka', split_axis=0, concat_axis=2, tiled=True)]
    ppermute x0 -> x3, starting transfers between devices: none -> 6.16 us  [end_values(): lax.ppermute(by_place[ii - 1], lane_axis, [(idx, (idx - 1) % n_all) for i...]
    dynamic_slice x6, local copies, waits for them, and re-layouts: 0.46 us -> 4.55 us  [one_block(): lax.dynamic_slice_in_dim(token_ids, q_start + begin_at, row_blk, 1)]
    all_to_all x1 -> x0, starting transfers between devices: 3.99 us -> none  [shards(): lax.all_to_all(bias_tile, 'ka', split_axis=0, concat_axis=2, tiled=True)]
    dot_general x6, matrix products: 6.08 us -> 2.41 us  [condition_block(): jnp.einsum('rkc,ch->hrk', normal_b, w_bias, preferred_element_type=jnp.fl...]
    all_to_all x1 -> x0, waiting for transfers between devices: 3.34 us -> none  [shards(): lax.all_to_all(bias_tile, 'ka', split_axis=0, concat_axis=2, tiled=True)]
  transfers between devices with their start and end apart: 3 -> 5, of which waited for: 2 -> 4; matrix products, arithmetic and copies ran while one was open for 41% -> 40% of each run, Pallas kernels for 0% -> 0%
where the time goes in v1:
time: 148 us; the launch traced here: 147 us
  matrix products  32.6 us (22%)
  waiting for transfers between devices  31.7 us (21%)
  other arithmetic  25.1 us (17%)
  local copies, waits for them, and re-layouts  24.3 us (16%)
  between operations  14.3 us (10%)
  blocking collectives  8.29 us (6%)
  starting transfers between devices  6.24 us (4%)
  loops' own time  4.99 us (3%)
    unnamed x3, waiting for transfers between devices  22.6 us
    ppermute x3, waiting for transfers between devices, end_values(): lax.ppermute(by_place[ii - 1], lane_axis, [(idx, (idx - 1) % n_all) for i...  9.12 us
    dot_general x12, matrix products, condition_block(): jnp.einsum('rkf,fc->rkc', hidden, trans_out[layer_idx], preferred_element...  8.85 us
    reduce_sum x24, other arithmetic, layer_norm(): spread = jnp.mean(centered * centered, axis=-1, keepdims=True)  8.39 us
    all_to_all x1, blocking collectives, shards(): lax.all_to_all(bias_tile, 'ka', split_axis=0, concat_axis=2, tiled=True)  8.29 us
    reduce_sum x12, other arithmetic, layer_norm(): average = jnp.mean(values, axis=-1, keepdims=True)  7.64 us
    ppermute x3, starting transfers between devices, end_values(): lax.ppermute(by_place[ii - 1], lane_axis, [(idx, (idx - 1) % n_all) for i...  6.16 us
    slice x2, local copies, waits for them, and re-layouts, shards(): keys_all = kv_all[:, 0].reshape(samples, heads_local, HD, kv_all.shape[3])  5.78 us
  transfers between devices with their start and end apart: 5, of which 4 were waited for; matrix products, arithmetic and copies ran while one was open for 40% of the time, Pallas kernels for 0%

profile of v1, /device:TPU:0, one launch (start us, length us, event | category | flops | bytes accessed | tf_op | source)
XLA Modules:
  0.0 147.4 jit_solution(1195766167117176327)
XLA Ops:
  7.2 2.5 %collective-permute-start = (bf16[8,48,192]{2,1,0:T(8,128)(2,1)}, bf16[8,48,192]{2,1,0:T(8,128)(2,1)S(1)}, u32[]{:S(2)}, u32[]{:S(2)}) collective-permute-start(bf16[8,48,192]{2,1,0:T(8,128)(2,1)} %param.25), channel_id=1, source_target_pairs={{0,3},{1,0},{2,1},{3,2},{4,7},{5,4},{6,5},{7,6},{8,11},{9,8},{10,9... | collective-permute-start | bytes 442376 | tf_op jit(solution)/shard_map/ppermute | solution.py:18
  9.7 3.5 %collective-permute-done = bf16[8,48,192]{2,1,0:T(8,128)(2,1)S(1)} collective-permute-done((bf16[8,48,192]{2,1,0:T(8,128)(2,1)}, bf16[8,48,192]{2,1,0:T(8,128)(2,1)S(1)}, u32[]{:S(2)}, u32[]{:S(2)}) %collective-permute-start) | collective-permute-done | bytes 147488 | tf_op jit(solution)/shard_map/ppermute | solution.py:18
  13.2 1.8 %collective-permute-start.1 = (bf16[8,48,192]{2,1,0:T(8,128)(2,1)S(1)}, bf16[8,48,192]{2,1,0:T(8,128)(2,1)S(1)}, u32[]{:S(2)}, u32[]{:S(2)}) collective-permute-start(bf16[8,48,192]{2,1,0:T(8,128)(2,1)S(1)} %collective-permute-done), channel_id=1, source_target_pairs={{0,3},{1,0},{2,1},{3,2},{4,7},{5,4},{6,5},{7,6},{8,11},{9,8},{10,9... | collective-permute-start | bytes 442376 | tf_op jit(solution)/shard_map/ppermute | solution.py:18
  15.0 3.2 %collective-permute-done.1 = bf16[8,48,192]{2,1,0:T(8,128)(2,1)S(1)} collective-permute-done((bf16[8,48,192]{2,1,0:T(8,128)(2,1)S(1)}, bf16[8,48,192]{2,1,0:T(8,128)(2,1)S(1)}, u32[]{:S(2)}, u32[]{:S(2)}) %collective-permute-start.1) | collective-permute-done | bytes 147488 | tf_op jit(solution)/shard_map/ppermute | solution.py:18
  18.2 1.9 %collective-permute-start.2 = (bf16[8,48,192]{2,1,0:T(8,128)(2,1)S(1)}, bf16[8,48,192]{2,1,0:T(8,128)(2,1)S(1)}, u32[]{:S(2)}, u32[]{:S(2)}) collective-permute-start(bf16[8,48,192]{2,1,0:T(8,128)(2,1)S(1)} %collective-permute-done.1), channel_id=1, source_target_pairs={{0,3},{1,0},{2,1},{3,2},{4,7},{5,4},{6,5},{7,6},{8,11},{9,8},{10,9... | collective-permute-start | bytes 442376 | tf_op jit(solution)/shard_map/ppermute | solution.py:18
  20.8 2.4 %collective-permute-done.2 = bf16[8,48,192]{2,1,0:T(8,128)(2,1)S(1)} collective-permute-done((bf16[8,48,192]{2,1,0:T(8,128)(2,1)S(1)}, bf16[8,48,192]{2,1,0:T(8,128)(2,1)S(1)}, u32[]{:S(2)}, u32[]{:S(2)}) %collective-permute-start.2) | collective-permute-done | bytes 147488 | tf_op jit(solution)/shard_map/ppermute | solution.py:18
  23.3 2.2 %concatenate.9 = bf16[8,48,1536]{2,1,0:T(8,128)(2,1)S(1)} concatenate(bf16[8,48,192]{2,1,0:T(8,128)(2,1)} %param.25, bf16[8,48,192]{2,1,0:T(8,128)(2,1)S(1)} %collective-permute-done, bf16[8,48,192]{2,1,0:T(8,128)(2,1)S(1)} %collective-permute-done.1, bf16[8,48,192]{2,1,0:T(8,128)(2,1)S(1)} %collective-permute-done.2, bf16[8,48,192]{2,1,0:T(8,128)(2,1)} %param.25, ...), dimensions={2} | concatenate | bytes 2359296 | tf_op jit(solution)/shard_map/jit(_roll_dynamic)/concatenate | solution.py:24
  25.5 2.0 %fusion.72 = (bf16[4,8,48,192]{3,2,0,1:T(8,128)(2,1)S(1)}, f32[4,8,48,192]{3,2,0,1:T(8,128)}) fusion(bf16[4,768,192]{1,2,0:T(8,128)(2,1)S(1)} %copy-done, bf16[8,48,1536]{2,1,0:T(8,128)(2,1)S(1)} %concatenate.9, s32[]{:T(128)S(6)} %select_n.46), kind=kOutput, calls=%fused_computation.120 | convolution fusion | flops 453279744 | bytes 3538948 | tf_op jit(solution)/shard_map/sqf,pfe->psqe/dot_general | solution.py:140
  28.6 60.8 %while.13 = (s32[]{:T(128)}, bf16[6,8,96,128]{3,2,1,0:T(8,128)(2,1)}, bf16[6,16,8,96]{3,1,2,0:T(8,128)(2,1)S(1)}, s32[6]{0:T(128)S(1)}, bf16[48,96,128]{2,1,0:T(...) while((s32[]{:T(128)}, ...), condition=%wide.region_10.11_spmd.clone, body=%wide.region_0.10_spmd.clone.sunk | while | flops 390749440 | bytes 14643635 | solution.py:131
  30.9 1.1 fusion.93
  36.7 1.0 bitcast_dynamic-update-slice_fusion.2
  41.0 1.1 fusion.93
  46.9 1.0 bitcast_dynamic-update-slice_fusion.2
  51.1 1.1 fusion.93
  57.0 1.0 bitcast_dynamic-update-slice_fusion.2
  61.3 1.1 fusion.93
  67.1 1.0 bitcast_dynamic-update-slice_fusion.2
  71.4 1.1 fusion.93
  77.3 1.0 bitcast_dynamic-update-slice_fusion.2
  81.6 1.1 fusion.93
  87.4 1.0 bitcast_dynamic-update-slice_fusion.2
  89.5 8.3 %all_to_all.4 = bf16[16,48,96]{2,1,0:T(8,128)(2,1)S(1)} all-to-all(bf16[16,48,96]{2,1,0:T(8,128)(2,1)S(1)} %bitcast.140), channel_id=1, replica_groups=mesh['pb'=8,'ka'=4] {'ka'}, dimensions={0} | all-to-all | bytes 294912 | tf_op jit(solution)/shard_map/all_to_all | solution.py:150
  98.3 1.0 convert_element_type.75
  99.3 1.1 fusion.56
  100.6 3.3 %fusion.70 = (bf16[8,1,192,384]{2,3,0,1:T(8,128)(2,1)}, bf16[8,1,192,384]{2,3,0,1:T(8,128)(2,1)S(1)}) fusion(bf16[8,2,192,384]{2,3,0,1:T(8,128)(2,1)} %all-gather.2.cloned.1.call-done), kind=kLoop, calls=%fused_computation.118 | loop fusion | bytes 4718592 | tf_op jit(solution)/shard_map/slice | solution.py:152
  103.9 2.5 %copy.29 = bf16[8,1,192,384]{3,2,0,1:T(8,128)(2,1)} copy(bf16[8,1,192,384]{2,3,0,1:T(8,128)(2,1)} %get-tuple-element.182) | data formatting | bytes 2359296 | tf_op jit(solution)/shard_map/slice | solution.py:152
  106.4 1.5 %copy.28 = bf16[8,1,192,384]{3,2,0,1:T(8,128)(2,1)} copy(bf16[8,1,192,384]{2,3,0,1:T(8,128)(2,1)S(1)} %get-tuple-element.183) | data formatting | bytes 2359296 | tf_op jit(solution)/shard_map/slice | solution.py:153
  107.9 3.7 %fusion.73 = (f32[8,4,48]{2,1,0:T(4,128)S(1)}, f32[8,4,48,384]{3,2,1,0:T(8,128)}) fusion(f32[4,48,384]{2,1,0:T(8,128)S(1)} %reshape.365, bf16[8,4,48,384]{3,2,1,0:T(8,128)(2,1)} %bitcast.138, bf16[8,48,4,48]{3,2,1,0:T(4,128)(2,1)} %convert_element_type.75), kind=kOutput, calls=%fused_computation.121 | convolution fusion | flops 58982784 | bytes 3987456 | tf_op jit(solution)/shard_map/sub | solution.py:85
  111.6 2.3 %convolution_bitcast_fusion.1 = f32[8,48,4,48]{1,3,2,0:T(8,128)S(1)} fusion(bf16[8,4,48,384]{3,2,1,0:T(8,128)(2,1)S(1)} %bitcast.139, f32[8,4,48,384]{3,2,1,0:T(8,128)} %get-tuple-element.190, f32[8,4,48]{2,1,0:T(4,128)S(1)} %get-tuple-element.189), kind=kOutput, calls=%fused_computation.93 | convolution fusion | flops 57802752 | bytes 3840000 | tf_op jit(solution)/shard_map/shqk,shdk->sqhd/dot_general | solution.py:160
  115.3 1.0 copy.36
  116.3 22.5 %reduce-scatter.4.cloned.1.call-done = bf16[192,384]{1,0:T(8,128)(2,1)} async-done(((bf16[768,384]{1,0:T(8,128)(2,1)}), bf16[192,384]{1,0:T(8,128)(2,1)}) %reduce-scatter.4.cloned.1.call-update) | async-done | bytes 147472
  138.8 1.7 %copy.37 = bf16[192,384]{0,1:T(8,128)(2,1)} copy(bf16[192,384]{1,0:T(8,128)(2,1)} %reduce-scatter.4.cloned.1.call-done) | data formatting | bytes 294912
  (221 shorter events, 47.1 us)
Async XLA Ops:
  7.2 18.4 %copy-start = (bf16[4,768,192]{1,2,0:T(8,128)(2,1)S(1)}, bf16[4,768,192]{1,2,0:T(8,128)(2,1)}, u32[]{:S(2)}) copy-start(bf16[4,768,192]{1,2,0:T(8,128)(2,1)} %param.26) | copy-start | bytes 3538948
  7.2 93.4 %all-gather.2.cloned.1.call-start = ((), (), s32[]{:S(2)}) async-start(), calls=%async_computation.2 | async-start | bytes 3538944 | tf_op jit(solution)/shard_map/all_gather | solution.py:151
  7.2 6.0 %collective-permute-start = (bf16[8,48,192]{2,1,0:T(8,128)(2,1)}, bf16[8,48,192]{2,1,0:T(8,128)(2,1)S(1)}, u32[]{:S(2)}, u32[]{:S(2)}) collective-permute-start(bf16[8,48,192]{2,1,0:T(8,128)(2,1)} %param.25), channel_id=1, source_target_pairs={{0,3},{1,0},{2,1},{3,2},{4,7},{5,4},{6,5},{7,6},{8,11},{9,8},{10,9... | collective-permute-start | bytes 442376 | tf_op jit(solution)/shard_map/ppermute | solution.py:18
  13.2 5.0 %collective-permute-start.1 = (bf16[8,48,192]{2,1,0:T(8,128)(2,1)S(1)}, bf16[8,48,192]{2,1,0:T(8,128)(2,1)S(1)}, u32[]{:S(2)}, u32[]{:S(2)}) collective-permute-start(bf16[8,48,192]{2,1,0:T(8,128)(2,1)S(1)} %collective-permute-done), channel_id=1, source_target_pairs={{0,3},{1,0},{2,1},{3,2},{4,7},{5,4},{6,5},{7,6},{8,11},{9,8},{10,9... | collective-permute-start | bytes 442376 | tf_op jit(solution)/shard_map/ppermute | solution.py:18
  18.2 5.1 %collective-permute-start.2 = (bf16[8,48,192]{2,1,0:T(8,128)(2,1)S(1)}, bf16[8,48,192]{2,1,0:T(8,128)(2,1)S(1)}, u32[]{:S(2)}, u32[]{:S(2)}) collective-permute-start(bf16[8,48,192]{2,1,0:T(8,128)(2,1)S(1)} %collective-permute-done.1), channel_id=1, source_target_pairs={{0,3},{1,0},{2,1},{3,2},{4,7},{5,4},{6,5},{7,6},{8,11},{9,8},{10,9... | collective-permute-start | bytes 442376 | tf_op jit(solution)/shard_map/ppermute | solution.py:18
  27.5 1.0 copy-start.1
  27.5 1.0 copy-start.4
  27.5 1.0 copy-start.5
  27.5 1.1 copy-start.6
  27.5 1.1 copy-start.7
  27.5 1.1 copy-start.8
  27.5 1.1 copy-start.9
  27.6 1.1 copy-start.10
  28.5 110.4 %reduce-scatter.4.cloned.1.call-start = ((), (), s32[]{:S(2)}) async-start(), calls=%async_computation.3 | async-start | bytes 737280
  107.9 3.7 %copy-start.2 = (bf16[8,1,192,384]{3,2,0,1:T(8,128)(2,1)S(1)}, bf16[8,1,192,384]{3,2,0,1:T(8,128)(2,1)}, u32[]{:S(2)}) copy-start(bf16[8,1,192,384]{3,2,0,1:T(8,128)(2,1)} %copy.28) | copy-start | bytes 3538948
  113.9 1.0 copy-start.3
Sparse Core Ops, SparseCore 0:
  28.6 61.6 all-gather.1
  116.4 22.3 reduce-scatter.3
